TPU v7x, 32 devices: a whole 2x2x4 slice. The times are simulated.
32 devices in a mesh: ctx: 8 (over y, x, core), dp: 4 (over z).
Axes of the slice: x: 2, y: 2, z: 4, core: 2. Of those that a mesh axis runs over, the one named last changes fastest.
Arguments:
- hidden_in: bfloat16 [4, 2048, 2048], P('dp', 'ctx'), may hold values from -6 to 6
- queries: bfloat16 [4, 2048, 2048], P('dp', 'ctx'), may hold values from -1000 to 1000
- norm_gain: bfloat16 [2048], replicated, may hold values from 0.099609375 to 1.8984375
- weight_store: bfloat16 [4, 2048, 512], P('dp', 'ctx'), may hold values from -0.125 to 0.125
- owners: int32 [2], replicated, may hold values from 0 to 3, as said below
- doc_lengths: int32 [4, 4], P('dp'), may hold values from 1 to 1024, 2048 in all within a row
Outputs:
- attended: bfloat16 [4, 2048, 2048], P('dp', 'ctx')
Inputs may be any that keep to these rules, and one draw needn't show every extreme that they name: `owners`: two different data ranks, one of them the last rank 4 - 1; the first owns the key projection, the second the value projection.
All inputs are finite; a program needn't handle non-finite values.
Results may differ from a plain program's by a relative error of at most 0.012.
Values may be sent and summed in bfloat16 or wider, within the bound.
No kernel may reach another device: no remote copies, remote signals or barrier semaphores. Data moves between devices by JAX's collectives and lax.ppermute only.
A program may use at most 64 MiB of HBM per device.

v0:
```python
import jax
import jax.numpy as jnp
from jax import lax
from jax.sharding import PartitionSpec as P

HS = 128
REACH = 4


def from_root(block, axis, owner):
    block = jnp.where(lax.axis_index(axis) == owner, block, jnp.zeros_like(block))
    return lax.psum(block, axis)


def from_behind(x, axis, by):
    size = lax.axis_size(axis)
    pairs = [(i, i + by) for i in range(size) if 0 <= i + by < size]
    return lax.ppermute(x, axis, pairs)


def find_starts(lengths, positions):
    ends = jnp.cumsum(lengths)
    starts = ends - lengths
    below = starts[None, :] <= positions[:, None]
    return jnp.max(jnp.where(below, starts[None, :], 0), axis=1)


def copy_owner(slot_rows, owner):
    return from_root(slot_rows, "dp", owner)


def local(hidden_in, queries, norm_gain, weight_store, owners, doc_lengths):
    tok_rows = hidden_in.shape[1]
    key_width = weight_store.shape[2]
    kv_heads = key_width // HS
    group = queries.shape[2] // key_width
    width_all = (REACH + 1) * tok_rows
    ctx_index = lax.axis_index("ctx")
    xf = hidden_in[0].astype(jnp.float32)
    scaled = (
        xf
        * lax.rsqrt(jnp.mean(xf * xf, axis=-1, keepdims=True) + 1e-05)
        * norm_gain.astype(jnp.float32)
    ).astype(jnp.bfloat16)
    own_slot = weight_store[0]
    key_part = copy_owner(own_slot, owners[0])
    value_part = copy_owner(own_slot, owners[1])
    key_sum = jnp.dot(
        scaled,
        lax.all_gather(key_part, "ctx", axis=0, tiled=True),
        preferred_element_type=jnp.float32,
    )
    value_sum = jnp.dot(
        scaled,
        lax.all_gather(value_part, "ctx", axis=0, tiled=True),
        preferred_element_type=jnp.float32,
    )
    kv_own = jnp.stack([key_sum.astype(jnp.bfloat16), value_sum.astype(jnp.bfloat16)])
    earlier = [from_behind(kv_own, "ctx", back) for back in range(REACH, 0, -1)]
    window = jnp.concatenate(earlier + [kv_own], axis=1)
    q_pos = ctx_index * tok_rows + jnp.arange(tok_rows, dtype=jnp.int32)
    k_pos = (ctx_index - REACH) * tok_rows + jnp.arange(width_all, dtype=jnp.int32)
    q_start = find_starts(doc_lengths[0], q_pos)
    allowed = (k_pos[None, :] >= q_start[:, None]) & (k_pos[None, :] <= q_pos[:, None])
    q_heads = jnp.transpose(queries[0].reshape(tok_rows, kv_heads, group, HS), (1, 2, 0, 3))
    k_heads = jnp.transpose(window[0].reshape(width_all, kv_heads, HS), (1, 0, 2))
    v_heads = jnp.transpose(window[1].reshape(width_all, kv_heads, HS), (1, 0, 2))
    inverse_root = 1.0 / jnp.sqrt(jnp.float32(HS))

    def one_head(args):
        q_one, k_one, v_one = args
        rows = q_one.reshape(group * tok_rows, HS)
        score = jnp.dot(rows, k_one.T, preferred_element_type=jnp.float32)
        score = score.reshape(group, tok_rows, width_all) * inverse_root
        score = jnp.where(allowed[None], score, jnp.float32(-1e30))
        top = jnp.max(score, axis=-1, keepdims=True)
        weight = jnp.exp(score - top)
        total = jnp.sum(weight, axis=-1)
        weight_b = weight.astype(jnp.bfloat16).reshape(group * tok_rows, width_all)
        summed = jnp.dot(weight_b, v_one, preferred_element_type=jnp.float32)
        summed = summed.reshape(group, tok_rows, HS)
        return (summed / total[..., None]).astype(jnp.bfloat16)

    outputs = lax.map(one_head, (q_heads, k_heads, v_heads))
    attended = jnp.transpose(outputs, (2, 0, 1, 3)).reshape(1, tok_rows, kv_heads * group * HS)
    return attended


def solution(mesh):
    return jax.shard_map(
        local,
        mesh=mesh,
        in_specs=(
            P("dp", "ctx", None),
            P("dp", "ctx", None),
            P(),
            P("dp", "ctx", None),
            P(),
            P("dp", None),
        ),
        out_specs=P("dp", "ctx", None),
        check_vma=False,
    )
```

profile of v0, /device:TPU:1, one launch (start us, length us, event | category | flops | bytes accessed | tf_op | source)
XLA Modules:
  0.0 198.7 jit_solution(8778680894563662250)
XLA Ops:
  6.5 1.4 fusion.36
  9.3 1.8 select_bitcast_fusion.1
  11.1 39.7 %all-reduce.3.cloned.1.call-done = (bf16[256,512]{1,0:T(8,128)(2,1)}, bf16[256,512]{1,0:T(8,128)(2,1)}) async-done(((bf16[256,512]{1,0:T(8,128)(2,1)}, bf16[256,512]{1,0:T(8,128)(2,1)}), (bf16[256,512]{1,0:T(8,128)(2,1)}, bf16[256,512]{1,0:T(8,128)(2,1)})) %all-reduce.3.cloned.1.call-update) | async-done | bytes 524304 | tf_op jit(solution)/shard_map/psum | solution.py:12
  53.4 28.6 %all-gather.3.cloned.1.call-done = bf16[2048,512]{1,0:T(8,128)(2,1)} async-done(((bf16[256,512]{1,0:T(8,128)(2,1)}), bf16[2048,512]{1,0:T(8,128)(2,1)}) %all-gather.3.cloned.1.call-update) | async-done | bytes 2097168 | tf_op jit(solution)/shard_map/all_gather | solution.py:50
  82.0 2.3 %fusion.30 = bf16[1,256,512]{2,1,0:T(8,128)(2,1)S(1)} fusion(bf16[2048,512]{1,0:T(8,128)(2,1)} %all-gather.3.cloned.1.call-done, bf16[1,256,2048]{2,1,0:T(8,128)(2,1)S(1)} %copy-done, f32[2048]{0:T(1024)S(1)} %convert_element_type.26, f32[256]{0:T(256)S(1)} %add_rsqrt_fusion), kind=kOutput, calls=%fused_computation.29 | convolution fusion | flops 539099136 | bytes 3417088 | tf_op jit(solution)/shard_map/dot_general | solution.py:48
  84.4 27.5 %all-gather.5.cloned.1.call-done = bf16[2048,512]{1,0:T(8,128)(2,1)} async-done(((bf16[256,512]{1,0:T(8,128)(2,1)}), bf16[2048,512]{1,0:T(8,128)(2,1)}) %all-gather.5.cloned.1.call-update) | async-done | bytes 2097168 | tf_op jit(solution)/shard_map/all_gather | solution.py:55
  111.8 2.3 %fusion.31 = bf16[1,256,512]{2,1,0:T(8,128)(2,1)S(1)} fusion(bf16[2048,512]{1,0:T(8,128)(2,1)} %all-gather.5.cloned.1.call-done, bf16[1,256,2048]{2,1,0:T(8,128)(2,1)S(1)} %copy-done, f32[2048]{0:T(1024)S(1)} %convert_element_type.26, f32[256]{0:T(256)S(1)} %add_rsqrt_fusion), kind=kOutput, calls=%fused_computation.30 | convolution fusion | flops 539099136 | bytes 3417088 | tf_op jit(solution)/shard_map/dot_general | solution.py:53
  115.7 3.8 %collective-permute-start = (bf16[2,256,512]{2,1,0:T(8,128)(2,1)}, bf16[2,256,512]{2,1,0:T(8,128)(2,1)}, u32[]{:S(2)}, u32[]{:S(2)}) collective-permute-start(bf16[2,256,512]{2,1,0:T(8,128)(2,1)} %pad_maximum_fusion), channel_id=1, source_target_pairs={{0,16},{4,20},{8,24},{12,28},{1,17},{5,21},{9,25},{13,29},{2,18},{... | collective-permute-start | bytes 1572872 | tf_op jit(solution)/shard_map/ppermute | solution.py:18
  119.5 2.1 %collective-permute-start.1 = (bf16[2,256,512]{2,1,0:T(8,128)(2,1)}, bf16[2,256,512]{2,1,0:T(8,128)(2,1)}, u32[]{:S(2)}, u32[]{:S(2)}) collective-permute-start(bf16[2,256,512]{2,1,0:T(8,128)(2,1)} %pad_maximum_fusion), channel_id=1, source_target_pairs={{0,12},{4,16},{8,20},{12,24},{16,28},{1,13},{5,17},{9,21},{13,25},... | collective-permute-start | bytes 1572872 | tf_op jit(solution)/shard_map/ppermute | solution.py:18
  121.6 2.9 %collective-permute-start.2 = (bf16[2,256,512]{2,1,0:T(8,128)(2,1)}, bf16[2,256,512]{2,1,0:T(8,128)(2,1)}, u32[]{:S(2)}, u32[]{:S(2)}) collective-permute-start(bf16[2,256,512]{2,1,0:T(8,128)(2,1)} %pad_maximum_fusion), channel_id=1, source_target_pairs={{0,8},{4,12},{8,16},{12,20},{16,24},{20,28},{1,9},{5,13},{9,17},{1... | collective-permute-start | bytes 1572872 | tf_op jit(solution)/shard_map/ppermute | solution.py:18
  124.5 1.9 collective-permute-start.3
  127.1 25.4 %collective-permute-done = bf16[2,256,512]{2,1,0:T(8,128)(2,1)} collective-permute-done((bf16[2,256,512]{2,1,0:T(8,128)(2,1)}, bf16[2,256,512]{2,1,0:T(8,128)(2,1)}, u32[]{:S(2)}, u32[]{:S(2)}) %collective-permute-start) | collective-permute-done | bytes 524320 | tf_op jit(solution)/shard_map/ppermute | solution.py:18
  152.5 1.1 constant_dynamic-update-slice_fusion.4
  153.6 5.2 %collective-permute-done.1 = bf16[2,256,512]{2,1,0:T(8,128)(2,1)} collective-permute-done((bf16[2,256,512]{2,1,0:T(8,128)(2,1)}, bf16[2,256,512]{2,1,0:T(8,128)(2,1)}, u32[]{:S(2)}, u32[]{:S(2)}) %collective-permute-start.1) | collective-permute-done | bytes 524320 | tf_op jit(solution)/shard_map/ppermute | solution.py:18
  158.8 1.1 constant_dynamic-update-slice_fusion.3
  159.9 1.1 constant_dynamic-update-slice_fusion.2
  161.0 1.1 constant_dynamic-update-slice_fusion.1
  162.1 1.2 fusion.35
  163.4 3.6 %reshape_squeeze.10 = bf16[1280,4,128]{2,1,0:T(4,128)(2,1)} reshape(bf16[1,1280,512]{2,1,0:T(8,128)(2,1)} %get-tuple-element.96) | data formatting | bytes 2621440 | tf_op jit(solution)/shard_map/reshape;squeeze | solution.py:66
  166.9 1.2 reshape_squeeze.11
  168.2 3.1 %copy_bitcast_fusion = (bf16[4,1280,128]{2,1,0:T(8,128)(2,1)}, bf16[4,1280,128]{2,1,0:T(8,128)(2,1)S(1)}) fusion(bf16[1280,4,128]{2,1,0:T(4,128)(2,1)} %reshape_squeeze.11, bf16[1280,4,128]{2,1,0:T(4,128)(2,1)} %reshape_squeeze.10), kind=kLoop, calls=%fused_computation.25 | loop fusion | bytes 5242880 | tf_op jit(solution)/shard_map/transpose | solution.py:67
  171.3 18.5 %while.11 = (s32[]{:T(128)}, bf16[4,4,256,128]{3,2,1,0:T(8,128)(2,1)S(1)}, bf16[4,4,256,128]{2,3,1,0:T(8,128)(2,1)S(1)}, bf16[4,1280,128]{2,1,0:T(8,128)(2,1)S(1...) while((s32[]{:T(128)}, ...), condition=%wide.region_8.9_spmd.clone, body=%wide.region_5.8_spmd.clone.sunk | while | flops 681506816 | bytes 17593436 | solution.py:84
  171.6 1.3 fusion.46
  172.9 1.0 fusion.47
  173.9 2.0 %fusion.48 = bf16[4,4,256,128]{3,2,1,0:T(8,128)(2,1)S(1)} fusion(bf16[4,4,256,128]{3,2,1,0:T(8,128)(2,1)S(1)} %get-tuple-element.166, s32[]{:T(128)} %get-tuple-element.165, f32[4,256,1280]{2,1,0:T(8,128)S(1)} %get-tuple-element.154, f32[4,256]{1,0:T(4,128)S(1)} %get-tuple-element.155, bf16[4,1280,128]{2,1,0:T(8,128)(2,1)} %get-tuple-element.178, ...), kind=kOutput, calls=%fused_computation.11.clone.1 | convolution fusion | flops 338427904 | bytes 5841920 | tf_op jit(solution)/shard_map/while/body/eval_jaxpr/dot_general | solution.py:80
  176.2 1.3 fusion.46
  178.5 2.0 %fusion.48 = bf16[4,4,256,128]{3,2,1,0:T(8,128)(2,1)S(1)} fusion(bf16[4,4,256,128]{3,2,1,0:T(8,128)(2,1)S(1)} %get-tuple-element.166, s32[]{:T(128)} %get-tuple-element.165, f32[4,256,1280]{2,1,0:T(8,128)S(1)} %get-tuple-element.154, f32[4,256]{1,0:T(4,128)S(1)} %get-tuple-element.155, bf16[4,1280,128]{2,1,0:T(8,128)(2,1)} %get-tuple-element.178, ...), kind=kOutput, calls=%fused_computation.11.clone.1 | convolution fusion | flops 338427904 | bytes 5841920 | tf_op jit(solution)/shard_map/while/body/eval_jaxpr/dot_general | solution.py:80
  180.8 1.3 fusion.46
  183.1 2.0 %fusion.48 = bf16[4,4,256,128]{3,2,1,0:T(8,128)(2,1)S(1)} fusion(bf16[4,4,256,128]{3,2,1,0:T(8,128)(2,1)S(1)} %get-tuple-element.166, s32[]{:T(128)} %get-tuple-element.165, f32[4,256,1280]{2,1,0:T(8,128)S(1)} %get-tuple-element.154, f32[4,256]{1,0:T(4,128)S(1)} %get-tuple-element.155, bf16[4,1280,128]{2,1,0:T(8,128)(2,1)} %get-tuple-element.178, ...), kind=kOutput, calls=%fused_computation.11.clone.1 | convolution fusion | flops 338427904 | bytes 5841920 | tf_op jit(solution)/shard_map/while/body/eval_jaxpr/dot_general | solution.py:80
  185.5 1.3 fusion.46
  187.7 2.0 %fusion.48 = bf16[4,4,256,128]{3,2,1,0:T(8,128)(2,1)S(1)} fusion(bf16[4,4,256,128]{3,2,1,0:T(8,128)(2,1)S(1)} %get-tuple-element.166, s32[]{:T(128)} %get-tuple-element.165, f32[4,256,1280]{2,1,0:T(8,128)S(1)} %get-tuple-element.154, f32[4,256]{1,0:T(4,128)S(1)} %get-tuple-element.155, bf16[4,1280,128]{2,1,0:T(8,128)(2,1)} %get-tuple-element.178, ...), kind=kOutput, calls=%fused_computation.11.clone.1 | convolution fusion | flops 338427904 | bytes 5841920 | tf_op jit(solution)/shard_map/while/body/eval_jaxpr/dot_general | solution.py:80
  190.6 1.6 reshape.47
  (38 shorter events, 9.8 us)
Async XLA Ops:
  6.5 46.5 %copy-start = (bf16[1,256,2048]{2,1,0:T(8,128)(2,1)S(1)}, bf16[1,256,2048]{2,1,0:T(8,128)(2,1)}, u32[]{:S(2)}) copy-start(bf16[1,256,2048]{2,1,0:T(8,128)(2,1)} %param.8) | copy-start | bytes 3145732
  6.5 44.3 %all-reduce.3.cloned.1.call-start = ((), (), s32[]{:S(2)}) async-start(), calls=%async_computation.2 | async-start | bytes 1048576 | tf_op jit(solution)/shard_map/psum | solution.py:12
  11.1 70.9 %all-gather.3.cloned.1.call-start = ((), (), s32[]{:S(2)}) async-start(), calls=%async_computation | async-start | bytes 2359296 | tf_op jit(solution)/shard_map/all_gather | solution.py:50
  50.8 61.0 %all-gather.5.cloned.1.call-start = ((), (), s32[]{:S(2)}) async-start(), calls=%async_computation.1 | async-start | bytes 2359296 | tf_op jit(solution)/shard_map/all_gather | solution.py:55
  84.3 37.3 %copy-start.4 = (s32[1,4]{1,0:T(1,128)S(1)}, s32[1,4]{1,0:T(1,128)}, u32[]{:S(2)}) copy-start(s32[1,4]{1,0:T(1,128)} %param.13) | copy-start | bytes 52
  84.3 42.1 %copy-start.1 = (bf16[1,256,2048]{2,1,0:T(8,128)(2,1)S(1)}, bf16[1,256,2048]{2,1,0:T(8,128)(2,1)}, u32[]{:S(2)}) copy-start(bf16[1,256,2048]{2,1,0:T(8,128)(2,1)} %param.9) | copy-start | bytes 3145732
  114.2 0.7 copy-start.2
  115.7 36.8 %collective-permute-start = (bf16[2,256,512]{2,1,0:T(8,128)(2,1)}, bf16[2,256,512]{2,1,0:T(8,128)(2,1)}, u32[]{:S(2)}, u32[]{:S(2)}) collective-permute-start(bf16[2,256,512]{2,1,0:T(8,128)(2,1)} %pad_maximum_fusion), channel_id=1, source_target_pairs={{0,16},{4,20},{8,24},{12,28},{1,17},{5,21},{9,25},{13,29},{2,18},{... | collective-permute-start | bytes 1572872 | tf_op jit(solution)/shard_map/ppermute | solution.py:18
  119.5 39.3 %collective-permute-start.1 = (bf16[2,256,512]{2,1,0:T(8,128)(2,1)}, bf16[2,256,512]{2,1,0:T(8,128)(2,1)}, u32[]{:S(2)}, u32[]{:S(2)}) collective-permute-start(bf16[2,256,512]{2,1,0:T(8,128)(2,1)} %pad_maximum_fusion), channel_id=1, source_target_pairs={{0,12},{4,16},{8,20},{12,24},{16,28},{1,13},{5,17},{9,21},{13,25},... | collective-permute-start | bytes 1572872 | tf_op jit(solution)/shard_map/ppermute | solution.py:18
  121.6 38.3 %collective-permute-start.2 = (bf16[2,256,512]{2,1,0:T(8,128)(2,1)}, bf16[2,256,512]{2,1,0:T(8,128)(2,1)}, u32[]{:S(2)}, u32[]{:S(2)}) collective-permute-start(bf16[2,256,512]{2,1,0:T(8,128)(2,1)} %pad_maximum_fusion), channel_id=1, source_target_pairs={{0,8},{4,12},{8,16},{12,20},{16,24},{20,28},{1,9},{5,13},{9,17},{1... | collective-permute-start | bytes 1572872 | tf_op jit(solution)/shard_map/ppermute | solution.py:18
  124.5 36.5 %collective-permute-start.3 = (bf16[2,256,512]{2,1,0:T(8,128)(2,1)}, bf16[2,256,512]{2,1,0:T(8,128)(2,1)}, u32[]{:S(2)}, u32[]{:S(2)}) collective-permute-start(bf16[2,256,512]{2,1,0:T(8,128)(2,1)} %pad_maximum_fusion), channel_id=1, source_target_pairs={{0,4},{4,8},{8,12},{12,16},{16,20},{20,24},{24,28},{1,5},{5,9},{9,... | collective-permute-start | bytes 1572872 | tf_op jit(solution)/shard_map/ppermute | solution.py:18
  127.1 35.0 %copy-start.3 = (bf16[1,256,512]{2,1,0:T(8,128)(2,1)S(1)}, bf16[1,256,512]{2,1,0:T(8,128)(2,1)}, u32[]{:S(2)}) copy-start(bf16[1,256,512]{2,1,0:T(8,128)(2,1)} %copy-done.2) | copy-start | bytes 786436
Sparse Core Ops, SparseCore 0:
  11.2 39.5 all-reduce.2
  52.7 29.2 all-gather.2
  83.9 27.8 all-gather.4
where the time goes:
time: 199 us
  waiting for transfers between devices  127 us (64%)
  local copies, waits for them, and re-layouts  18.5 us (9%)
  matrix products  17.9 us (9%)
  between operations  14.6 us (7%)
  starting transfers between devices  10.8 us (5%)
  other arithmetic  9.72 us (5%)
    psum x1, waiting for transfers between devices, from_root(): return lax.psum(block, axis)  39.7 us
    ppermute x4, waiting for transfers between devices, from_behind(): return lax.ppermute(x, axis, pairs)  30.6 us
    all_gather x1, waiting for transfers between devices, local(): lax.all_gather(key_part, 'ctx', axis=0, tiled=True)  28.6 us
    all_gather x1, waiting for transfers between devices, local(): lax.all_gather(value_part, 'ctx', axis=0, tiled=True)  27.5 us
    ppermute x4, starting transfers between devices, from_behind(): return lax.ppermute(x, axis, pairs)  10.7 us
    dot_general x4, matrix products, one_head(): summed = jnp.dot(weight_b, v_one, preferred_element_type=jnp.float32)  8.07 us
    unnamed x15, local copies, waits for them, and re-layouts  5.55 us
    dot_general x4, matrix products, one_head(): score = jnp.dot(rows, k_one.T, preferred_element_type=jnp.float32)  5.14 us
  transfers between devices with their start and end apart: 7, of which 5 were waited for; matrix products, arithmetic and copies ran while one was open for 4% of the time, Pallas kernels for 0%

commit v1 on v0

--- a/solution.py
+++ b/solution.py
@@ -5,6 +5,28 @@
 
 HS = 128
 REACH = 4
+
+
+def joined_along(pieces, dim):
+    pieces = jnp.moveaxis(pieces, 0, dim)
+    shape = pieces.shape
+    return pieces.reshape(*shape[:dim], shape[dim] * shape[dim + 1], *shape[dim + 2 :])
+
+
+def ring_gather(array, axis, dim):
+    size = lax.axis_size(axis)
+    pairs = [(i, (i + 1) % size) for i in range(size)]
+    back = [(b, a) for a, b in pairs]
+    lower, upper = ([], [])
+    for step in range(size - 1):
+        if step % 2 == 0:
+            lower.append(lax.ppermute(lower[-1] if lower else array, axis, pairs))
+        else:
+            upper.append(lax.ppermute(upper[-1] if upper else array, axis, back))
+    blocks = jnp.stack([*lower[::-1], array, *upper])
+    shift = lax.axis_index(axis) - len(lower)
+    blocks = blocks[(jnp.arange(size) - shift) % size]
+    return joined_along(blocks, dim)
 
 
 def from_root(block, axis, owner):
@@ -51,9 +73,7 @@
         preferred_element_type=jnp.float32,
     )
     value_sum = jnp.dot(
-        scaled,
-        lax.all_gather(value_part, "ctx", axis=0, tiled=True),
-        preferred_element_type=jnp.float32,
+        scaled, ring_gather(value_part, "ctx", 0), preferred_element_type=jnp.float32
     )
     kv_own = jnp.stack([key_sum.astype(jnp.bfloat16), value_sum.astype(jnp.bfloat16)])
     earlier = [from_behind(kv_own, "ctx", back) for back in range(REACH, 0, -1)]

time: 199 us -> 183 us (0.920)
  waiting for transfers between devices: 127 us -> 87 us
  starting transfers between devices: 10.8 us -> 28.9 us
  local copies, waits for them, and re-layouts: 18.5 us -> 24.7 us
    all_gather x1, waiting for transfers between devices: 28.6 us -> 0.02 us  [local(): lax.all_gather(key_part, 'ctx', axis=0, tiled=True)]
    all_gather x1 -> x0, waiting for transfers between devices: 27.5 us -> none  [local(): lax.all_gather(value_part, 'ctx', axis=0, tiled=True)]
    ppermute x0 -> x7, waiting for transfers between devices: none -> 21.1 us  [the longest x4 11.2 us: ring_gather(): lower.append(lax.ppermute(lower[-1] if lower else array, axis, pairs))]
    ppermute x0 -> x7, starting transfers between devices: none -> 12.9 us  [the longest x4 10.2 us: ring_gather(): lower.append(lax.ppermute(lower[-1] if lower else array, axis, pairs))]
    ppermute x4, starting transfers between devices: 10.7 us -> 16 us  [from_behind(): return lax.ppermute(x, axis, pairs)]
    ppermute x4, waiting for transfers between devices: 30.6 us -> 26.2 us  [from_behind(): return lax.ppermute(x, axis, pairs)]
    unnamed x15 -> x40, local copies, waits for them, and re-layouts: 5.55 us -> 9.81 us
  transfers between devices with their start and end apart: 7 -> 13, of which waited for: 5 -> 9; matrix products, arithmetic and copies ran while one was open for 4% -> 7% of each run, Pallas kernels for 0% -> 0%
where the time goes in v1:
time: 183 us; the launch traced here: 182 us
  waiting for transfers between devices  87 us (48%)
  starting transfers between devices  28.9 us (16%)
  local copies, waits for them, and re-layouts  24.7 us (13%)
  matrix products  18 us (10%)
  between operations  15 us (8%)
  other arithmetic  8.44 us (5%)
    psum x1, waiting for transfers between devices, from_root(): return lax.psum(block, axis)  39.7 us
    ppermute x4, waiting for transfers between devices, from_behind(): return lax.ppermute(x, axis, pairs)  26.2 us
    ppermute x4, starting transfers between devices, from_behind(): return lax.ppermute(x, axis, pairs)  16 us
    ppermute x4, waiting for transfers between devices, ring_gather(): lower.append(lax.ppermute(lower[-1] if lower else array, axis, pairs))  11.2 us
    ppermute x4, starting transfers between devices, ring_gather(): lower.append(lax.ppermute(lower[-1] if lower else array, axis, pairs))  10.2 us
    ppermute x3, waiting for transfers between devices, ring_gather(): upper.append(lax.ppermute(upper[-1] if upper else array, axis, back))  9.88 us
    unnamed x40, local copies, waits for them, and re-layouts  9.81 us
    dot_general x4, matrix products, one_head(): summed = jnp.dot(weight_b, v_one, preferred_element_type=jnp.float32)  8.07 us
  transfers between devices with their start and end apart: 13, of which 9 were waited for; matrix products, arithmetic and copies ran while one was open for 7% of the time, Pallas kernels for 0%

profile of v1, /device:TPU:1, one launch (start us, length us, event | category | flops | bytes accessed | tf_op | source)
XLA Modules:
  0.0 182.2 jit_solution(14895654219731491559)
XLA Ops:
  6.5 1.4 fusion.47
  9.2 1.8 select_bitcast_fusion.1
  11.0 39.7 %all-reduce.3.cloned.1.call-done = (bf16[256,512]{1,0:T(8,128)(2,1)}, bf16[256,512]{1,0:T(8,128)(2,1)}) async-done(((bf16[256,512]{1,0:T(8,128)(2,1)}, bf16[256,512]{1,0:T(8,128)(2,1)}), (bf16[256,512]{1,0:T(8,128)(2,1)}, bf16[256,512]{1,0:T(8,128)(2,1)})) %all-reduce.3.cloned.1.call-update) | async-done | bytes 524304 | tf_op jit(solution)/shard_map/psum | solution.py:34
  50.7 2.8 %collective-permute-start = (bf16[256,512]{1,0:T(8,128)(2,1)}, bf16[256,512]{1,0:T(8,128)(2,1)S(1)}, u32[]{:S(2)}, u32[]{:S(2)}) collective-permute-start(bf16[256,512]{1,0:T(8,128)(2,1)} %get-tuple-element.91), channel_id=1, source_target_pairs={{0,4},{4,8},{8,12},{12,16},{16,20},{20,24},{24,28},{28,0},{1,5},{5... | collective-permute-start | bytes 786440 | tf_op jit(solution)/shard_map/ppermute | solution.py:23
  53.6 3.6 %collective-permute-done = bf16[256,512]{1,0:T(8,128)(2,1)S(1)} collective-permute-done((bf16[256,512]{1,0:T(8,128)(2,1)}, bf16[256,512]{1,0:T(8,128)(2,1)S(1)}, u32[]{:S(2)}, u32[]{:S(2)}) %collective-permute-start) | collective-permute-done | bytes 262176 | tf_op jit(solution)/shard_map/ppermute | solution.py:23
  57.2 2.4 %collective-permute-start.1 = (bf16[256,512]{1,0:T(8,128)(2,1)S(1)}, bf16[256,512]{1,0:T(8,128)(2,1)S(1)}, u32[]{:S(2)}, u32[]{:S(2)}) collective-permute-start(bf16[256,512]{1,0:T(8,128)(2,1)S(1)} %collective-permute-done), channel_id=1, source_target_pairs={{0,4},{4,8},{8,12},{12,16},{16,20},{20,24},{24,28},{28,0},{1,5},{5... | collective-permute-start | bytes 786440 | tf_op jit(solution)/shard_map/ppermute | solution.py:23
  59.6 6.3 %collective-permute-done.1 = bf16[256,512]{1,0:T(8,128)(2,1)S(1)} collective-permute-done((bf16[256,512]{1,0:T(8,128)(2,1)S(1)}, bf16[256,512]{1,0:T(8,128)(2,1)S(1)}, u32[]{:S(2)}, u32[]{:S(2)}) %collective-permute-start.1) | collective-permute-done | bytes 262176 | tf_op jit(solution)/shard_map/ppermute | solution.py:23
  65.8 2.5 %collective-permute-start.2 = (bf16[256,512]{1,0:T(8,128)(2,1)S(1)}, bf16[256,512]{1,0:T(8,128)(2,1)S(1)}, u32[]{:S(2)}, u32[]{:S(2)}) collective-permute-start(bf16[256,512]{1,0:T(8,128)(2,1)S(1)} %collective-permute-done.1), channel_id=1, source_target_pairs={{0,4},{4,8},{8,12},{12,16},{16,20},{20,24},{24,28},{28,0},{1,5},{5... | collective-permute-start | bytes 786440 | tf_op jit(solution)/shard_map/ppermute | solution.py:23
  68.6 2.4 %collective-permute-done.4 = bf16[256,512]{1,0:T(8,128)(2,1)S(1)} collective-permute-done((bf16[256,512]{1,0:T(8,128)(2,1)}, bf16[256,512]{1,0:T(8,128)(2,1)S(1)}, u32[]{:S(2)}, u32[]{:S(2)}) %collective-permute-start.4) | collective-permute-done | bytes 262176 | tf_op jit(solution)/shard_map/ppermute | solution.py:25
  71.6 2.5 %collective-permute-start.3 = (bf16[256,512]{1,0:T(8,128)(2,1)S(1)}, bf16[256,512]{1,0:T(8,128)(2,1)}, u32[]{:S(2)}, u32[]{:S(2)}) collective-permute-start(bf16[256,512]{1,0:T(8,128)(2,1)S(1)} %collective-permute-done.2), channel_id=1, source_target_pairs={{0,4},{4,8},{8,12},{12,16},{16,20},{20,24},{24,28},{28,0},{1,5},{5... | collective-permute-start | bytes 786440 | tf_op jit(solution)/shard_map/ppermute | solution.py:23
  74.3 7.5 %collective-permute-done.5 = bf16[256,512]{1,0:T(8,128)(2,1)} collective-permute-done((bf16[256,512]{1,0:T(8,128)(2,1)S(1)}, bf16[256,512]{1,0:T(8,128)(2,1)}, u32[]{:S(2)}, u32[]{:S(2)}) %collective-permute-start.5) | collective-permute-done | bytes 262176 | tf_op jit(solution)/shard_map/ppermute | solution.py:25
  81.8 2.7 %collective-permute-start.6 = (bf16[256,512]{1,0:T(8,128)(2,1)}, bf16[256,512]{1,0:T(8,128)(2,1)S(1)}, u32[]{:S(2)}, u32[]{:S(2)}) collective-permute-start(bf16[256,512]{1,0:T(8,128)(2,1)} %collective-permute-done.5), channel_id=1, source_target_pairs={{4,0},{8,4},{12,8},{16,12},{20,16},{24,20},{28,24},{0,28},{5,1},{9... | collective-permute-start | bytes 786440 | tf_op jit(solution)/shard_map/ppermute | solution.py:25
  90.3 2.0 %gather_fusion = bf16[8,256,512]{2,1,0:T(8,128)(2,1)} fusion(bf16[8,256,512]{2,1,0:T(8,128)(2,1)S(1)} %bitcast_dynamic-update-slice_fusion, s32[1024]{0:T(1024)S(1)} %pad_clamp_fusion), kind=kCustom, calls=%fused_computation | custom fusion | bytes 4194336 | tf_op jit(solution)/shard_map/gather | solution.py:28
  92.3 2.3 %fusion.35 = bf16[1,256,512]{2,1,0:T(8,128)(2,1)S(1)} fusion(bf16[2048,512]{1,0:T(8,128)(2,1)} %bitcast.86, bf16[1,256,2048]{2,1,0:T(8,128)(2,1)S(1)} %copy-done, f32[2048]{0:T(1024)S(1)} %convert_element_type.34, f32[256]{0:T(256)S(1)} %add_rsqrt_fusion), kind=kOutput, calls=%fused_computation.35 | convolution fusion | flops 539099136 | bytes 3417088 | tf_op jit(solution)/shard_map/dot_general | solution.py:75
  94.7 2.5 %fusion.34 = bf16[1,256,512]{2,1,0:T(8,128)(2,1)S(1)} fusion(bf16[2048,512]{1,0:T(8,128)(2,1)} %all-gather.2.cloned.1.call-done, bf16[1,256,2048]{2,1,0:T(8,128)(2,1)S(1)} %copy-done, f32[2048]{0:T(1024)S(1)} %convert_element_type.34, f32[256]{0:T(256)S(1)} %add_rsqrt_fusion), kind=kOutput, calls=%fused_computation.34 | convolution fusion | flops 539099136 | bytes 3417088 | tf_op jit(solution)/shard_map/dot_general | solution.py:70
  98.0 4.6 %collective-permute-start.7 = (bf16[2,256,512]{2,1,0:T(8,128)(2,1)}, bf16[2,256,512]{2,1,0:T(8,128)(2,1)}, u32[]{:S(2)}, u32[]{:S(2)}) collective-permute-start(bf16[2,256,512]{2,1,0:T(8,128)(2,1)} %pad_maximum_fusion), channel_id=1, source_target_pairs={{0,16},{4,20},{8,24},{12,28},{1,17},{5,21},{9,25},{13,29},{2,18},{... | collective-permute-start | bytes 1572872 | tf_op jit(solution)/shard_map/ppermute | solution.py:40
  102.6 6.8 %collective-permute-start.8 = (bf16[2,256,512]{2,1,0:T(8,128)(2,1)}, bf16[2,256,512]{2,1,0:T(8,128)(2,1)}, u32[]{:S(2)}, u32[]{:S(2)}) collective-permute-start(bf16[2,256,512]{2,1,0:T(8,128)(2,1)} %pad_maximum_fusion), channel_id=1, source_target_pairs={{0,12},{4,16},{8,20},{12,24},{16,28},{1,13},{5,17},{9,21},{13,25},... | collective-permute-start | bytes 1572872 | tf_op jit(solution)/shard_map/ppermute | solution.py:40
  109.5 2.1 %collective-permute-start.9 = (bf16[2,256,512]{2,1,0:T(8,128)(2,1)}, bf16[2,256,512]{2,1,0:T(8,128)(2,1)}, u32[]{:S(2)}, u32[]{:S(2)}) collective-permute-start(bf16[2,256,512]{2,1,0:T(8,128)(2,1)} %pad_maximum_fusion), channel_id=1, source_target_pairs={{0,8},{4,12},{8,16},{12,20},{16,24},{20,28},{1,9},{5,13},{9,17},{1... | collective-permute-start | bytes 1572872 | tf_op jit(solution)/shard_map/ppermute | solution.py:40
  111.6 2.5 %collective-permute-start.10 = (bf16[2,256,512]{2,1,0:T(8,128)(2,1)}, bf16[2,256,512]{2,1,0:T(8,128)(2,1)}, u32[]{:S(2)}, u32[]{:S(2)}) collective-permute-start(bf16[2,256,512]{2,1,0:T(8,128)(2,1)} %pad_maximum_fusion), channel_id=1, source_target_pairs={{0,4},{4,8},{8,12},{12,16},{16,20},{20,24},{24,28},{1,5},{5,9},{9,... | collective-permute-start | bytes 1572872 | tf_op jit(solution)/shard_map/ppermute | solution.py:40
  114.7 18.2 %collective-permute-done.7 = bf16[2,256,512]{2,1,0:T(8,128)(2,1)} collective-permute-done((bf16[2,256,512]{2,1,0:T(8,128)(2,1)}, bf16[2,256,512]{2,1,0:T(8,128)(2,1)}, u32[]{:S(2)}, u32[]{:S(2)}) %collective-permute-start.7) | collective-permute-done | bytes 524320 | tf_op jit(solution)/shard_map/ppermute | solution.py:40
  133.9 8.0 %collective-permute-done.8 = bf16[2,256,512]{2,1,0:T(8,128)(2,1)} collective-permute-done((bf16[2,256,512]{2,1,0:T(8,128)(2,1)}, bf16[2,256,512]{2,1,0:T(8,128)(2,1)}, u32[]{:S(2)}, u32[]{:S(2)}) %collective-permute-start.8) | collective-permute-done | bytes 524320 | tf_op jit(solution)/shard_map/ppermute | solution.py:40
  146.5 3.6 %reshape_squeeze.10 = bf16[1280,4,128]{2,1,0:T(4,128)(2,1)} reshape(bf16[1,1280,512]{2,1,0:T(8,128)(2,1)} %get-tuple-element.96) | data formatting | bytes 2621440 | tf_op jit(solution)/shard_map/reshape;squeeze | solution.py:86
  151.3 3.1 %copy_bitcast_fusion = (bf16[4,1280,128]{2,1,0:T(8,128)(2,1)}, bf16[4,1280,128]{2,1,0:T(8,128)(2,1)S(1)}) fusion(bf16[1280,4,128]{2,1,0:T(4,128)(2,1)} %reshape_squeeze.11, bf16[1280,4,128]{2,1,0:T(4,128)(2,1)} %reshape_squeeze.10), kind=kLoop, calls=%fused_computation.30 | loop fusion | bytes 5242880 | tf_op jit(solution)/shard_map/transpose | solution.py:87
  154.4 18.5 %while.11 = (s32[]{:T(128)}, bf16[4,4,256,128]{3,2,1,0:T(8,128)(2,1)S(1)}, bf16[4,4,256,128]{2,3,1,0:T(8,128)(2,1)S(1)}, bf16[4,1280,128]{2,1,0:T(8,128)(2,1)S(1...) while((s32[]{:T(128)}, ...), condition=%wide.region_8.9_spmd.clone, body=%wide.region_5.8_spmd.clone.sunk | while | flops 681506816 | bytes 17593436 | solution.py:104
  157.0 2.0 %fusion.59 = bf16[4,4,256,128]{3,2,1,0:T(8,128)(2,1)S(1)} fusion(bf16[4,4,256,128]{3,2,1,0:T(8,128)(2,1)S(1)} %get-tuple-element.166, s32[]{:T(128)} %get-tuple-element.165, f32[4,256,1280]{2,1,0:T(8,128)S(1)} %get-tuple-element.154, f32[4,256]{1,0:T(4,128)S(1)} %get-tuple-element.155, bf16[4,1280,128]{2,1,0:T(8,128)(2,1)} %get-tuple-element.178, ...), kind=kOutput, calls=%fused_computation.12.clone.1 | convolution fusion | flops 338427904 | bytes 5841920 | tf_op jit(solution)/shard_map/while/body/eval_jaxpr/dot_general | solution.py:100
  159.4 1.3 fusion.57
  161.6 2.0 %fusion.59 = bf16[4,4,256,128]{3,2,1,0:T(8,128)(2,1)S(1)} fusion(bf16[4,4,256,128]{3,2,1,0:T(8,128)(2,1)S(1)} %get-tuple-element.166, s32[]{:T(128)} %get-tuple-element.165, f32[4,256,1280]{2,1,0:T(8,128)S(1)} %get-tuple-element.154, f32[4,256]{1,0:T(4,128)S(1)} %get-tuple-element.155, bf16[4,1280,128]{2,1,0:T(8,128)(2,1)} %get-tuple-element.178, ...), kind=kOutput, calls=%fused_computation.12.clone.1 | convolution fusion | flops 338427904 | bytes 5841920 | tf_op jit(solution)/shard_map/while/body/eval_jaxpr/dot_general | solution.py:100
  164.0 1.3 fusion.57
  166.2 2.0 %fusion.59 = bf16[4,4,256,128]{3,2,1,0:T(8,128)(2,1)S(1)} fusion(bf16[4,4,256,128]{3,2,1,0:T(8,128)(2,1)S(1)} %get-tuple-element.166, s32[]{:T(128)} %get-tuple-element.165, f32[4,256,1280]{2,1,0:T(8,128)S(1)} %get-tuple-element.154, f32[4,256]{1,0:T(4,128)S(1)} %get-tuple-element.155, bf16[4,1280,128]{2,1,0:T(8,128)(2,1)} %get-tuple-element.178, ...), kind=kOutput, calls=%fused_computation.12.clone.1 | convolution fusion | flops 338427904 | bytes 5841920 | tf_op jit(solution)/shard_map/while/body/eval_jaxpr/dot_general | solution.py:100
  168.6 1.3 fusion.57
  170.9 2.0 %fusion.59 = bf16[4,4,256,128]{3,2,1,0:T(8,128)(2,1)S(1)} fusion(bf16[4,4,256,128]{3,2,1,0:T(8,128)(2,1)S(1)} %get-tuple-element.166, s32[]{:T(128)} %get-tuple-element.165, f32[4,256,1280]{2,1,0:T(8,128)S(1)} %get-tuple-element.154, f32[4,256]{1,0:T(4,128)S(1)} %get-tuple-element.155, bf16[4,1280,128]{2,1,0:T(8,128)(2,1)} %get-tuple-element.178, ...), kind=kOutput, calls=%fused_computation.12.clone.1 | convolution fusion | flops 338427904 | bytes 5841920 | tf_op jit(solution)/shard_map/while/body/eval_jaxpr/dot_general | solution.py:100
  173.7 1.6 reshape.113
  (78 shorter events, 22.5 us)
Async XLA Ops:
  6.5 61.8 %copy-start = (bf16[1,256,2048]{2,1,0:T(8,128)(2,1)S(1)}, bf16[1,256,2048]{2,1,0:T(8,128)(2,1)}, u32[]{:S(2)}) copy-start(bf16[1,256,2048]{2,1,0:T(8,128)(2,1)} %param.8) | copy-start | bytes 3145732
  6.5 67.6 %copy-start.12 = (bf16[2048]{0:T(1024)(128)(2,1)S(1)}, bf16[2048]{0:T(1024)(128)(2,1)}, u32[]{:S(2)}) copy-start(bf16[2048]{0:T(1024)(128)(2,1)} %param.10) | copy-start | bytes 12292
  6.5 67.6 %copy-start.13 = (s32[1,4]{1,0:T(1,128)S(1)}, s32[1,4]{1,0:T(1,128)}, u32[]{:S(2)}) copy-start(s32[1,4]{1,0:T(1,128)} %param.13) | copy-start | bytes 52
  6.5 44.2 %all-reduce.3.cloned.1.call-start = ((), (), s32[]{:S(2)}) async-start(), calls=%async_computation.1 | async-start | bytes 1048576 | tf_op jit(solution)/shard_map/psum | solution.py:34
  11.0 83.7 %all-gather.2.cloned.1.call-start = ((), (), s32[]{:S(2)}) async-start(), calls=%async_computation | async-start | bytes 2359296 | tf_op jit(solution)/shard_map/all_gather | solution.py:72
  50.7 38.5 %copy-start.6 = (bf16[256,512]{1,0:T(8,128)(2,1)S(1)}, bf16[256,512]{1,0:T(8,128)(2,1)}, u32[]{:S(2)}) copy-start(bf16[256,512]{1,0:T(8,128)(2,1)} %get-tuple-element.91) | copy-start | bytes 786436
  50.7 6.5 %collective-permute-start = (bf16[256,512]{1,0:T(8,128)(2,1)}, bf16[256,512]{1,0:T(8,128)(2,1)S(1)}, u32[]{:S(2)}, u32[]{:S(2)}) collective-permute-start(bf16[256,512]{1,0:T(8,128)(2,1)} %get-tuple-element.91), channel_id=1, source_target_pairs={{0,4},{4,8},{8,12},{12,16},{16,20},{20,24},{24,28},{28,0},{1,5},{5... | collective-permute-start | bytes 786440 | tf_op jit(solution)/shard_map/ppermute | solution.py:23
  57.2 27.3 %copy-start.7 = (bf16[256,512]{1,0:T(8,128)(2,1)}, bf16[256,512]{1,0:T(8,128)(2,1)S(1)}, u32[]{:S(2)}) copy-start(bf16[256,512]{1,0:T(8,128)(2,1)S(1)} %collective-permute-done) | copy-start | bytes 786436
  57.2 8.6 %collective-permute-start.1 = (bf16[256,512]{1,0:T(8,128)(2,1)S(1)}, bf16[256,512]{1,0:T(8,128)(2,1)S(1)}, u32[]{:S(2)}, u32[]{:S(2)}) collective-permute-start(bf16[256,512]{1,0:T(8,128)(2,1)S(1)} %collective-permute-done), channel_id=1, source_target_pairs={{0,4},{4,8},{8,12},{12,16},{16,20},{20,24},{24,28},{28,0},{1,5},{5... | collective-permute-start | bytes 786440 | tf_op jit(solution)/shard_map/ppermute | solution.py:23
  59.6 11.5 %collective-permute-start.4 = (bf16[256,512]{1,0:T(8,128)(2,1)}, bf16[256,512]{1,0:T(8,128)(2,1)S(1)}, u32[]{:S(2)}, u32[]{:S(2)}) collective-permute-start(bf16[256,512]{1,0:T(8,128)(2,1)} %get-tuple-element.91), channel_id=1, source_target_pairs={{4,0},{8,4},{12,8},{16,12},{20,16},{24,20},{28,24},{0,28},{5,1},{9... | collective-permute-start | bytes 786440 | tf_op jit(solution)/shard_map/ppermute | solution.py:25
  65.8 18.7 %copy-start.8 = (bf16[256,512]{1,0:T(8,128)(2,1)}, bf16[256,512]{1,0:T(8,128)(2,1)S(1)}, u32[]{:S(2)}) copy-start(bf16[256,512]{1,0:T(8,128)(2,1)S(1)} %collective-permute-done.1) | copy-start | bytes 786436
  65.8 5.8 %collective-permute-start.2 = (bf16[256,512]{1,0:T(8,128)(2,1)S(1)}, bf16[256,512]{1,0:T(8,128)(2,1)S(1)}, u32[]{:S(2)}, u32[]{:S(2)}) collective-permute-start(bf16[256,512]{1,0:T(8,128)(2,1)S(1)} %collective-permute-done.1), channel_id=1, source_target_pairs={{0,4},{4,8},{8,12},{12,16},{16,20},{20,24},{24,28},{28,0},{1,5},{5... | collective-permute-start | bytes 786440 | tf_op jit(solution)/shard_map/ppermute | solution.py:23
  71.0 13.5 %copy-start.9 = (bf16[256,512]{1,0:T(8,128)(2,1)}, bf16[256,512]{1,0:T(8,128)(2,1)S(1)}, u32[]{:S(2)}) copy-start(bf16[256,512]{1,0:T(8,128)(2,1)S(1)} %collective-permute-done.4) | copy-start | bytes 786436
  71.0 10.8 %collective-permute-start.5 = (bf16[256,512]{1,0:T(8,128)(2,1)S(1)}, bf16[256,512]{1,0:T(8,128)(2,1)}, u32[]{:S(2)}, u32[]{:S(2)}) collective-permute-start(bf16[256,512]{1,0:T(8,128)(2,1)S(1)} %collective-permute-done.4), channel_id=1, source_target_pairs={{4,0},{8,4},{12,8},{16,12},{20,16},{24,20},{28,24},{0,28},{5,1},{9... | collective-permute-start | bytes 786440 | tf_op jit(solution)/shard_map/ppermute | solution.py:25
  71.6 12.9 %copy-start.11 = (bf16[256,512]{1,0:T(8,128)(2,1)}, bf16[256,512]{1,0:T(8,128)(2,1)S(1)}, u32[]{:S(2)}) copy-start(bf16[256,512]{1,0:T(8,128)(2,1)S(1)} %collective-permute-done.2) | copy-start | bytes 786436
  71.6 13.7 %collective-permute-start.3 = (bf16[256,512]{1,0:T(8,128)(2,1)S(1)}, bf16[256,512]{1,0:T(8,128)(2,1)}, u32[]{:S(2)}, u32[]{:S(2)}) collective-permute-start(bf16[256,512]{1,0:T(8,128)(2,1)S(1)} %collective-permute-done.2), channel_id=1, source_target_pairs={{0,4},{4,8},{8,12},{12,16},{16,20},{20,24},{24,28},{28,0},{1,5},{5... | collective-permute-start | bytes 786440 | tf_op jit(solution)/shard_map/ppermute | solution.py:23
  81.8 8.5 %collective-permute-start.6 = (bf16[256,512]{1,0:T(8,128)(2,1)}, bf16[256,512]{1,0:T(8,128)(2,1)S(1)}, u32[]{:S(2)}, u32[]{:S(2)}) collective-permute-start(bf16[256,512]{1,0:T(8,128)(2,1)} %collective-permute-done.5), channel_id=1, source_target_pairs={{4,0},{8,4},{12,8},{16,12},{20,16},{24,20},{28,24},{0,28},{5,1},{9... | collective-permute-start | bytes 786440 | tf_op jit(solution)/shard_map/ppermute | solution.py:25
  85.3 4.0 %copy-start.10 = (bf16[256,512]{1,0:T(8,128)(2,1)S(1)}, bf16[256,512]{1,0:T(8,128)(2,1)}, u32[]{:S(2)}) copy-start(bf16[256,512]{1,0:T(8,128)(2,1)} %copy-done.9) | copy-start | bytes 786436
  94.6 2.5 %copy-start.2 = (bf16[1,256,512]{2,1,0:T(8,128)(2,1)}, bf16[1,256,512]{2,1,0:T(8,128)(2,1)S(1)}, u32[]{:S(2)}) copy-start(bf16[1,256,512]{2,1,0:T(8,128)(2,1)S(1)} %fusion.35) | copy-start | bytes 786436
  94.6 19.4 %copy-start.1 = (bf16[1,256,2048]{2,1,0:T(8,128)(2,1)S(1)}, bf16[1,256,2048]{2,1,0:T(8,128)(2,1)}, u32[]{:S(2)}) copy-start(bf16[1,256,2048]{2,1,0:T(8,128)(2,1)} %param.9) | copy-start | bytes 3145732
  97.2 16.9 %copy-start.4 = (bf16[1,256,512]{2,1,0:T(8,128)(2,1)}, bf16[1,256,512]{2,1,0:T(8,128)(2,1)S(1)}, u32[]{:S(2)}) copy-start(bf16[1,256,512]{2,1,0:T(8,128)(2,1)S(1)} %fusion.34) | copy-start | bytes 786436
  98.0 34.8 %collective-permute-start.7 = (bf16[2,256,512]{2,1,0:T(8,128)(2,1)}, bf16[2,256,512]{2,1,0:T(8,128)(2,1)}, u32[]{:S(2)}, u32[]{:S(2)}) collective-permute-start(bf16[2,256,512]{2,1,0:T(8,128)(2,1)} %pad_maximum_fusion), channel_id=1, source_target_pairs={{0,16},{4,20},{8,24},{12,28},{1,17},{5,21},{9,25},{13,29},{2,18},{... | collective-permute-start | bytes 1572872 | tf_op jit(solution)/shard_map/ppermute | solution.py:40
  102.6 39.3 %collective-permute-start.8 = (bf16[2,256,512]{2,1,0:T(8,128)(2,1)}, bf16[2,256,512]{2,1,0:T(8,128)(2,1)}, u32[]{:S(2)}, u32[]{:S(2)}) collective-permute-start(bf16[2,256,512]{2,1,0:T(8,128)(2,1)} %pad_maximum_fusion), channel_id=1, source_target_pairs={{0,12},{4,16},{8,20},{12,24},{16,28},{1,13},{5,17},{9,21},{13,25},... | collective-permute-start | bytes 1572872 | tf_op jit(solution)/shard_map/ppermute | solution.py:40
  109.5 33.6 %collective-permute-start.9 = (bf16[2,256,512]{2,1,0:T(8,128)(2,1)}, bf16[2,256,512]{2,1,0:T(8,128)(2,1)}, u32[]{:S(2)}, u32[]{:S(2)}) collective-permute-start(bf16[2,256,512]{2,1,0:T(8,128)(2,1)} %pad_maximum_fusion), channel_id=1, source_target_pairs={{0,8},{4,12},{8,16},{12,20},{16,24},{20,28},{1,9},{5,13},{9,17},{1... | collective-permute-start | bytes 1572872 | tf_op jit(solution)/shard_map/ppermute | solution.py:40
  111.6 32.6 %collective-permute-start.10 = (bf16[2,256,512]{2,1,0:T(8,128)(2,1)}, bf16[2,256,512]{2,1,0:T(8,128)(2,1)}, u32[]{:S(2)}, u32[]{:S(2)}) collective-permute-start(bf16[2,256,512]{2,1,0:T(8,128)(2,1)} %pad_maximum_fusion), channel_id=1, source_target_pairs={{0,4},{4,8},{8,12},{12,16},{16,20},{20,24},{24,28},{1,5},{5,9},{9,... | collective-permute-start | bytes 1572872 | tf_op jit(solution)/shard_map/ppermute | solution.py:40
  114.7 30.5 %copy-start.3 = (bf16[1,256,512]{2,1,0:T(8,128)(2,1)S(1)}, bf16[1,256,512]{2,1,0:T(8,128)(2,1)}, u32[]{:S(2)}) copy-start(bf16[1,256,512]{2,1,0:T(8,128)(2,1)} %copy-done.2) | copy-start | bytes 786436
  114.7 30.5 %copy-start.5 = (bf16[1,256,512]{2,1,0:T(8,128)(2,1)S(1)}, bf16[1,256,512]{2,1,0:T(8,128)(2,1)}, u32[]{:S(2)}) copy-start(bf16[1,256,512]{2,1,0:T(8,128)(2,1)} %copy-done.4) | copy-start | bytes 786436
Sparse Core Ops, SparseCore 0:
  11.1 39.5 all-reduce.2
  52.6 34.6 all-gather.1
